TPU v7x, 256 devices: a whole 4x4x8 slice. The times are simulated.
256 devices in a mesh: tm: 4 (over x), rows: 64 (over y, z, core).
Axes of the slice: x: 4, y: 4, z: 8, core: 2. Of those that a mesh axis runs over, the one named last changes fastest.
Arguments:
- latent: bfloat16 [4, 64, 160, 512], P('tm', 'rows'), may hold values from -350 to 350, as said below
- norm_gain: float32 [512], replicated, may hold values from 0.1 to 1.9
- norm_bias: float32 [512], replicated, may hold values from -4 to 4
- conv_weight: bfloat16 [3, 3, 3, 512, 512], P(None, None, None, 'rows', 'tm'), may hold values from -0.0546875 to 0.0546875
- cotangent: bfloat16 [4, 128, 320, 512], P('tm', 'rows'), may hold values from -180 to 180
Outputs:
- latent_grad: float32 [4, 64, 160, 512], P('tm', 'rows')
- gain_grad: float32 [512], replicated
- bias_grad: float32 [512], replicated
Inputs may be any that keep to these rules, and one draw needn't show every extreme that they name: `latent`: features of the unit's input.
All inputs are finite; a program needn't handle non-finite values.
Results may differ from a plain program's by a relative error of at most 0.0003.
Values may be sent and summed in bfloat16 or wider, within the bound.
No kernel may reach another device: no remote copies, remote signals or barrier semaphores. Data moves between devices by JAX's collectives and lax.ppermute only.
A program may use at most 320 MiB of HBM per device.

v0:
```python
import jax
import jax.numpy as jnp
from jax import lax
from jax.sharding import PartitionSpec as P

GROUPS = 32


def extended(block, sides, width):
    for axis, dim in sides:
        count = lax.axis_size(axis)
        forward = [(i, i + 1) for i in range(count - 1)]
        backward = [(target, source) for source, target in forward]
        low = lax.ppermute(
            lax.slice_in_dim(block, block.shape[dim] - width, None, axis=dim), axis, forward
        )
        high = lax.ppermute(lax.slice_in_dim(block, 0, width, axis=dim), axis, backward)
        block = jnp.concatenate([low, block, high], axis=dim)
    return block


def from_behind(value, axis, steps):
    count = lax.axis_size(axis)
    first, last = (max(0, -steps), min(count, count - steps))
    return lax.ppermute(value, axis, [(source, source + steps) for source in range(first, last)])


def shifted_rows(frames, extra_frames):
    padded = jnp.pad(frames, ((0, extra_frames), (0, 0), (1, 1), (0, 0)))
    fine_rows = frames.shape[1] - 2
    return [padded[:, 2 - row_tap : 2 - row_tap + fine_rows] for row_tap in range(3)]


def tap_total(row_slabs, weights, tap_pairs, frames_out, span_cols):
    running = None
    for offset, tap_index in tap_pairs:
        for row_tap in range(3):
            source = row_slabs[row_tap][offset : offset + frames_out]
            for col_tap in range(3):
                product = lax.dot_general(
                    source,
                    weights[tap_index, row_tap, col_tap],
                    (((3,), (1,)), ((), ())),
                    preferred_element_type=jnp.float32,
                )
                piece = product[:, :, 2 - col_tap : 2 - col_tap + span_cols, :]
                running = piece if running is None else running + piece
    return running


def pool_pairs(fine_grad):
    frames, fine_rows, span_cols, channels = fine_grad.shape
    return fine_grad.reshape(frames, fine_rows // 2, 2, span_cols // 2, 2, channels).sum(
        axis=(2, 4)
    )


def block_grad(row_slabs, weights, frames_out, first_frame):
    span_cols = row_slabs[0].shape[2] - 2

    def extra_terms():
        return tap_total(row_slabs, weights, ((0, 1), (0, 0), (1, 0)), 1, span_cols)

    def no_terms():
        return jnp.zeros((1, row_slabs[0].shape[1], span_cols, weights.shape[3]), jnp.float32)

    main_part = tap_total(row_slabs, weights, ((0, 2), (1, 1), (2, 0)), frames_out, span_cols)
    main_part = main_part + lax.cond(first_frame, extra_terms, no_terms)
    return pool_pairs(main_part)


def on_device(latent, norm_gain, norm_bias, conv_weight, cotangent):
    frames_all = lax.axis_size("tm")
    rows_all = lax.axis_size("rows")
    low_rows = latent.shape[1]
    low_cols = latent.shape[2]
    channels = latent.shape[3]
    per_group = channels // GROUPS
    cell_count = frames_all * rows_all * low_rows * low_cols
    rimmed = extended(cotangent, (("rows", 1),), 1)
    following = from_behind(rimmed, "tm", -1)
    further = from_behind(rimmed, "tm", -2)
    stacked = jnp.concatenate([rimmed, following, further], axis=0)
    weight_wide = lax.all_gather(conv_weight, "tm", axis=4, tiled=True)
    weight_full = lax.all_gather(weight_wide, "rows", axis=3, tiled=True)
    up_grad = block_grad(shifted_rows(stacked, 0), weight_full, 1, lax.axis_index("tm") == 0)
    features = latent.astype(jnp.float32)
    sum_x = jnp.sum(features, axis=(0, 1, 2))
    sum_sq = jnp.sum(features * features, axis=(0, 1, 2))
    total_x, total_sq = lax.psum((sum_x, sum_sq), ("tm", "rows"))
    group_x = total_x.reshape(GROUPS, per_group).sum(axis=1)
    group_sq = total_sq.reshape(GROUPS, per_group).sum(axis=1)
    group_mean = group_x / (cell_count * per_group)
    group_var = group_sq / (cell_count * per_group) - group_mean * group_mean
    inv_std = lax.rsqrt(group_var + 1e-06)
    mean_chan = jnp.repeat(group_mean, per_group)
    inv_chan = jnp.repeat(inv_std, per_group)
    normed = (features - mean_chan) * inv_chan
    pre = normed * norm_gain + norm_bias
    sigmoid_pre = jax.nn.sigmoid(pre)
    act_grad = up_grad * sigmoid_pre * (1.0 + pre * (1.0 - sigmoid_pre))
    sum_act, sum_scaled = lax.psum(
        (jnp.sum(act_grad, axis=(0, 1, 2)), jnp.sum(act_grad * normed, axis=(0, 1, 2))),
        ("tm", "rows"),
    )
    gain_grad = sum_scaled / cell_count
    bias_grad = sum_act / cell_count
    mean_q = (norm_gain * sum_act).reshape(GROUPS, per_group).sum(axis=1) / (cell_count * per_group)
    mean_qn = (norm_gain * sum_scaled).reshape(GROUPS, per_group).sum(axis=1) / (
        cell_count * per_group
    )
    latent_grad = inv_chan * (
        act_grad * norm_gain
        - jnp.repeat(mean_q, per_group)
        - normed * jnp.repeat(mean_qn, per_group)
    )
    return (latent_grad, gain_grad, bias_grad)


def solution(mesh):
    placed = (
        P("tm", "rows", None, None),
        P(),
        P(),
        P(None, None, None, "rows", "tm"),
        P("tm", "rows", None, None),
    )
    return jax.shard_map(
        on_device,
        mesh=mesh,
        in_specs=placed,
        out_specs=(P("tm", "rows", None, None), P(), P()),
        check_vma=False,
    )
```

profile of v0, /device:TPU:1, one launch (start us, length us, event | category | flops | bytes accessed | tf_op | source)
XLA Modules:
  0.0 354.6 jit_solution(4041163253013684087)
XLA Ops:
  7.2 11.7 %all_gather.6 = bf16[3,3,3,8,512]{4,3,2,1,0:T(8,128)(2,1)} all-gather(bf16[3,3,3,8,128]{4,3,2,1,0:T(8,128)(2,1)} %param.10), channel_id=1, replica_groups=mesh['tm'=4,'rows'=64] {'tm'}, dimensions={4}, use_global_device_ids=true | all-gather | bytes 276480 | tf_op jit(solution)/shard_map/all_gather | solution.py:84
  20.1 6.2 %collective-permute-start = (bf16[1,1,320,512]{3,2,1,0:T(8,128)(2,1)S(1)}, bf16[1,1,320,512]{3,2,1,0:T(8,128)(2,1)S(1)}, u32[]{:S(2)}, u32[]{:S(2)}) collective-permute-start(bf16[1,1,320,512]{3,2,1,0:T(8,128)(2,1)S(1)} %get-tuple-element.27), channel_id=1, source_target_pairs={{0,1},{1,2},{2,3},{3,4},{4,5},{5,6},{6,7},{7,8},{8,9},{9,10},{10,1... | collective-permute-start | bytes 983048 | tf_op jit(solution)/shard_map/ppermute | solution.py:14
  26.3 1.9 collective-permute-start.1
  28.2 2.1 collective-permute-done
  30.4 4.3 %collective-permute-done.1 = bf16[1,1,320,512]{3,2,1,0:T(8,128)(2,1)S(1)} collective-permute-done((bf16[1,1,320,512]{3,2,1,0:T(8,128)(2,1)S(1)}, bf16[1,1,320,512]{3,2,1,0:T(8,128)(2,1)S(1)}, u32[]{:S(2)}, u32[]{:S(2)}) %collective-permute-start.1) | collective-permute-done | bytes 327712 | tf_op jit(solution)/shard_map/ppermute | solution.py:17
  37.6 129.7 %all-reduce.2 = (f32[32,16]{1,0:T(8,128)S(1)}, f32[32,16]{1,0:T(8,128)S(1)}) all-reduce(f32[32,16]{1,0:T(8,128)S(1)} %reshape.178, f32[32,16]{1,0:T(8,128)S(1)} %reshape.177), channel_id=1, replica_groups=mesh['tm'=4,'rows'=64] {'tm','rows'}, use_global_device_ids=true, to_apply=%region_4.5 | all-reduce | flops 1024 | bytes 8192 | tf_op jit(solution)/shard_map/psum | solution.py:90
  167.8 3.9 %fusion.113 = bf16[3,4,322,512]{3,2,1,0:T(8,128)(2,1)} fusion(bf16[1,4,320,512]{3,2,1,0:T(8,128)(2,1)} %collective-permute-done.3, bf16[1,4,320,512]{3,2,1,0:T(8,128)(2,1)} %collective-permute-done.2, bf16[1,4,320,512]{3,2,1,0:T(8,128)(2,1)S(1)} %constant_dynamic-update-slice_fusion), kind=kLoop, calls=%fused_computation.168 | loop fusion | flops 23740416 | bytes 7888896 | tf_op jit(solution)/shard_map/concatenate | solution.py:83
  171.7 48.1 %conditional.1 = (f32[1,2,320,512]{3,2,1,0:T(8,128)}) conditional(s32[]{:T(128)} %convert_element_type.9, () %tuple.14, (bf16[3,4,322,512]{3,2,1,0:T(8,128)(2,1)}, bf16[3,3,3,512,512]{4,3,2,1,0:T(8,128)(2,1)}) %tuple.15), branch_computations={%region_6.7_spmd, %region_7.8_spmd} | conditional | flops 9124839424 | bytes 177053760 | solution.py:68
  171.7 1.9 convolution_bitcast_fusion.15
  173.6 1.8 convolution_bitcast_fusion.16
  175.5 1.7 convolution_bitcast_fusion.17
  177.2 2.0 convolution_bitcast_fusion.24
  179.2 2.1 convolution_bitcast_fusion.25
  202.4 1.7 convolution_bitcast_fusion.5
  204.1 1.7 convolution_bitcast_fusion.8
  210.7 9.0 %slice_add_fusion = f32[1,2,320,512]{3,2,1,0:T(8,128)} fusion(f32[1,2,322,512]{3,2,1,0:T(8,128)} %convolution_bitcast_fusion, f32[1,2,322,512]{3,2,1,0:T(8,128)} %convolution_bitcast_fusion.1, f32[1,2,322,512]{3,2,1,0:T(8,128)} %convolution_bitcast_fusion.2, f32[1,2,322,512]{3,2,1,0:T(8,128)} %convolution_bitcast_fusion.3, ...), kind=kLoop, calls=%fused_computation.27 | loop fusion | flops 8519680 | bytes 36700160 | tf_op jit(solution)/shard_map/cond/branch_1_fun/add | solution.py:47
  219.8 1.9 convolution_bitcast_fusion.28
  221.7 1.8 convolution_bitcast_fusion.27
  223.6 1.7 convolution_bitcast_fusion.31
  225.3 2.0 convolution_bitcast_fusion.30
  227.3 2.1 convolution_bitcast_fusion.34
  237.0 1.7 convolution_bitcast_fusion.45
  259.9 10.1 %fusion.115 = f32[320,512]{1,0:T(8,128)} fusion(f32[1,2,320,512]{3,2,1,0:T(8,128)} %get-tuple-element.34, f32[1,2,322,512]{3,2,1,0:T(8,128)S(1)} %convolution_bitcast_fusion.27, f32[1,2,322,512]{3,2,1,0:T(8,128)S(1)} %convolution_bitcast_fusion.28, f32[1,2,322,512]{3,2,1,0:T(8,128)} %convolution_bitcast_fusion.29, ...), kind=kLoop, calls=%fused_computation.198 | loop fusion | flops 9011200 | bytes 37355520 | tf_op jit(solution)/shard_map/reduce_sum | solution.py:53
  272.5 73.1 %all-reduce.1 = (f32[512]{0:T(512)S(1)}, f32[512]{0:T(512)S(1)}) all-reduce(f32[512]{0:T(512)S(1)} %get-tuple-element.18, f32[512]{0:T(512)S(1)} %get-tuple-element.17), channel_id=1, replica_groups=mesh['tm'=4,'rows'=64] {'tm','rows'}, use_global_device_ids=true, to_apply=%region_14.15 | all-reduce | flops 1024 | bytes 8192 | tf_op jit(solution)/shard_map/psum | solution.py:102
  (93 shorter events, 63.8 us)
Async XLA Ops:
  7.2 23.2 %copy-start.4 = (bf16[1,2,320,512]{3,2,1,0:T(8,128)(2,1)S(1)}, bf16[1,2,320,512]{3,2,1,0:T(8,128)(2,1)}, u32[]{:S(2)}) copy-start(bf16[1,2,320,512]{3,2,1,0:T(8,128)(2,1)} %param.11) | copy-start | bytes 1966084
  7.2 164.5 %all-gather.2.cloned.1.call-start = ((), (), s32[]{:S(2)}) async-start(), calls=%async_computation | async-start | bytes 14376960 | tf_op jit(solution)/shard_map/all_gather | solution.py:85
  20.0 17.3 %copy-start.5 = (bf16[1,1,160,512]{3,2,1,0:T(8,128)(2,1)S(1)}, bf16[1,1,160,512]{3,2,1,0:T(8,128)(2,1)}, u32[]{:S(2)}) copy-start(bf16[1,1,160,512]{3,2,1,0:T(8,128)(2,1)} %param.7) | copy-start | bytes 491524
  20.1 10.2 %collective-permute-start = (bf16[1,1,320,512]{3,2,1,0:T(8,128)(2,1)S(1)}, bf16[1,1,320,512]{3,2,1,0:T(8,128)(2,1)S(1)}, u32[]{:S(2)}, u32[]{:S(2)}) collective-permute-start(bf16[1,1,320,512]{3,2,1,0:T(8,128)(2,1)S(1)} %get-tuple-element.27), channel_id=1, source_target_pairs={{0,1},{1,2},{2,3},{3,4},{4,5},{5,6},{6,7},{7,8},{8,9},{9,10},{10,1... | collective-permute-start | bytes 983048 | tf_op jit(solution)/shard_map/ppermute | solution.py:14
  26.3 8.4 %collective-permute-start.1 = (bf16[1,1,320,512]{3,2,1,0:T(8,128)(2,1)S(1)}, bf16[1,1,320,512]{3,2,1,0:T(8,128)(2,1)S(1)}, u32[]{:S(2)}, u32[]{:S(2)}) collective-permute-start(bf16[1,1,320,512]{3,2,1,0:T(8,128)(2,1)S(1)} %get-tuple-element.26), channel_id=1, source_target_pairs={{1,0},{2,1},{3,2},{4,3},{5,4},{6,5},{7,6},{8,7},{9,8},{10,9},{11,1... | collective-permute-start | bytes 983048 | tf_op jit(solution)/shard_map/ppermute | solution.py:17
  34.7 133.1 %collective-permute-start.3 = (bf16[1,4,320,512]{3,2,1,0:T(8,128)(2,1)S(1)}, bf16[1,4,320,512]{3,2,1,0:T(8,128)(2,1)}, u32[]{:S(2)}, u32[]{:S(2)}) collective-permute-start(bf16[1,4,320,512]{3,2,1,0:T(8,128)(2,1)S(1)} %constant_dynamic-update-slice_fusion), channel_id=1, source_target_pairs={{128,0},{192,64},{129,1},{193,65},{130,2},{194,66},{131,3},{195,67... | collective-permute-start | bytes 3932168 | tf_op jit(solution)/shard_map/ppermute | solution.py:25
  36.0 131.8 %collective-permute-start.2 = (bf16[1,4,320,512]{3,2,1,0:T(8,128)(2,1)S(1)}, bf16[1,4,320,512]{3,2,1,0:T(8,128)(2,1)}, u32[]{:S(2)}, u32[]{:S(2)}) collective-permute-start(bf16[1,4,320,512]{3,2,1,0:T(8,128)(2,1)S(1)} %constant_dynamic-update-slice_fusion), channel_id=1, source_target_pairs={{64,0},{128,64},{192,128},{65,1},{129,65},{193,129},{66,2},{130,66... | collective-permute-start | bytes 3932168 | tf_op jit(solution)/shard_map/ppermute | solution.py:25
  171.7 3.7 %copy-start.1 = (bf16[3,4,322,512]{3,2,1,0:T(8,128)(2,1)S(1)}, bf16[3,4,322,512]{3,2,1,0:T(8,128)(2,1)}, u32[]{:S(2)}) copy-start(bf16[3,4,322,512]{3,2,1,0:T(8,128)(2,1)} %get-tuple-element.12) | copy-start | bytes 11870212 | tf_op jit(solution)/shard_map/cond
  175.4 10.7 %copy-start.3 = (bf16[3,3,3,512,512]{4,3,2,1,0:T(8,128)(2,1)S(1)}, bf16[3,3,3,512,512]{4,3,2,1,0:T(8,128)(2,1)}, u32[]{:S(2)}) copy-start(bf16[3,3,3,512,512]{4,3,2,1,0:T(8,128)(2,1)} %get-tuple-element.13) | copy-start | bytes 42467332 | tf_op jit(solution)/shard_map/cond
  219.8 3.7 %copy-start = (bf16[3,4,322,512]{3,2,1,0:T(8,128)(2,1)S(1)}, bf16[3,4,322,512]{3,2,1,0:T(8,128)(2,1)}, u32[]{:S(2)}) copy-start(bf16[3,4,322,512]{3,2,1,0:T(8,128)(2,1)} %fusion.113) | copy-start | bytes 11870212
  223.5 10.7 %copy-start.2 = (bf16[3,3,3,512,512]{4,3,2,1,0:T(8,128)(2,1)S(1)}, bf16[3,3,3,512,512]{4,3,2,1,0:T(8,128)(2,1)}, u32[]{:S(2)}) copy-start(bf16[3,3,3,512,512]{4,3,2,1,0:T(8,128)(2,1)} %all-gather.2.cloned.1.call-done) | copy-start | bytes 42467332
  270.0 2.3 copy-start.6
  270.0 2.3 copy-start.7
Sparse Core Ops, SparseCore 0:
  19.0 105.3 all-gather.1
where the time goes:
time: 355 us
  blocking collectives  214 us (60%)
  matrix products  78.8 us (22%)
  other arithmetic  26 us (7%)
  between operations  14.3 us (4%)
  starting transfers between devices  10.8 us (3%)
  waiting for transfers between devices  6.41 us (2%)
  local copies, waits for them, and re-layouts  3.66 us (1%)
    psum x1, blocking collectives, on_device(): total_x, total_sq = lax.psum((sum_x, sum_sq), ('tm', 'rows'))  130 us
    dot_general x54, matrix products, tap_total(): lax.dot_general(source, weights[tap_index, row_tap, col_tap], (((3,), (1,...  78.8 us
    psum x1, blocking collectives, on_device(): lax.psum((jnp.sum(act_grad, axis=(0, 1, 2)), jnp.sum(act_grad * normed, a...  73.1 us
    all_gather x1, blocking collectives, on_device(): weight_wide = lax.all_gather(conv_weight, 'tm', axis=4, tiled=True)  11.7 us
    reduce_sum x2, other arithmetic, pool_pairs(): fine_grad.reshape(frames, fine_rows // 2, 2, span_cols // 2, 2, channels)  10.9 us
    add x1, other arithmetic, tap_total(): running = piece if running is None else running + piece  9.05 us
  transfers between devices with their start and end apart: 5, of which 2 were waited for; matrix products, arithmetic and copies ran while one was open for 2% of the time, Pallas kernels for 0%

commit v1 on v0

--- a/solution.py
+++ b/solution.py
@@ -100,8 +100,10 @@
     sigmoid_pre = jax.nn.sigmoid(pre)
     act_grad = up_grad * sigmoid_pre * (1.0 + pre * (1.0 - sigmoid_pre))
     sum_act, sum_scaled = lax.psum(
-        (jnp.sum(act_grad, axis=(0, 1, 2)), jnp.sum(act_grad * normed, axis=(0, 1, 2))),
-        ("tm", "rows"),
+        lax.psum(
+            (jnp.sum(act_grad, axis=(0, 1, 2)), jnp.sum(act_grad * normed, axis=(0, 1, 2))), "tm"
+        ),
+        "rows",
     )
     gain_grad = sum_scaled / cell_count
     bias_grad = sum_act / cell_count

time: 355 us -> 414 us (1.17)
  blocking collectives: 214 us -> 273 us
    psum x0 -> x1, blocking collectives: none -> 126 us  [on_device(): lax.psum(lax.psum((jnp.sum(act_grad, axis=(0, 1, 2)), jnp.sum(act_grad *...]
    psum x1, blocking collectives: 73.1 us -> 6 us  [on_device(): lax.psum((jnp.sum(act_grad, axis=(0, 1, 2)), jnp.sum(act_grad * normed, a...]
  transfers between devices with their start and end apart: 5 -> 5, of which waited for: 2 -> 2; matrix products, arithmetic and copies ran while one was open for 2% -> 1% of each run, Pallas kernels for 0% -> 0%
where the time goes in v1:
time: 414 us; the launch traced here: 413 us
  blocking collectives  273 us (66%)
  matrix products  78.8 us (19%)
  other arithmetic  26 us (6%)
  between operations  14.3 us (3%)
  starting transfers between devices  10.8 us (3%)
  waiting for transfers between devices  6.41 us (2%)
    psum x1, blocking collectives, on_device(): total_x, total_sq = lax.psum((sum_x, sum_sq), ('tm', 'rows'))  130 us
    psum x1, blocking collectives, on_device(): lax.psum(lax.psum((jnp.sum(act_grad, axis=(0, 1, 2)), jnp.sum(act_grad *...  126 us
    dot_general x54, matrix products, tap_total(): lax.dot_general(source, weights[tap_index, row_tap, col_tap], (((3,), (1,...  78.8 us
    all_gather x1, blocking collectives, on_device(): weight_wide = lax.all_gather(conv_weight, 'tm', axis=4, tiled=True)  11.7 us
    reduce_sum x2, other arithmetic, pool_pairs(): fine_grad.reshape(frames, fine_rows // 2, 2, span_cols // 2, 2, channels)  10.9 us
    add x1, other arithmetic, tap_total(): running = piece if running is None else running + piece  9.05 us
  transfers between devices with their start and end apart: 5, of which 2 were waited for; matrix products, arithmetic and copies ran while one was open for 1% of the time, Pallas kernels for 0%

profile of v1, /device:TPU:1, one launch (start us, length us, event | category | flops | bytes accessed | tf_op | source)
XLA Modules:
  0.0 413.3 jit_solution(13539322158960216465)
XLA Ops:
  7.2 11.7 %all_gather.6 = bf16[3,3,3,8,512]{4,3,2,1,0:T(8,128)(2,1)} all-gather(bf16[3,3,3,8,128]{4,3,2,1,0:T(8,128)(2,1)} %param.10), channel_id=1, replica_groups=mesh['tm'=4,'rows'=64] {'tm'}, dimensions={4}, use_global_device_ids=true | all-gather | bytes 276480 | tf_op jit(solution)/shard_map/all_gather | solution.py:84
  20.1 6.2 %collective-permute-start = (bf16[1,1,320,512]{3,2,1,0:T(8,128)(2,1)S(1)}, bf16[1,1,320,512]{3,2,1,0:T(8,128)(2,1)S(1)}, u32[]{:S(2)}, u32[]{:S(2)}) collective-permute-start(bf16[1,1,320,512]{3,2,1,0:T(8,128)(2,1)S(1)} %get-tuple-element.29), channel_id=1, source_target_pairs={{0,1},{1,2},{2,3},{3,4},{4,5},{5,6},{6,7},{7,8},{8,9},{9,10},{10,1... | collective-permute-start | bytes 983048 | tf_op jit(solution)/shard_map/ppermute | solution.py:14
  26.3 1.9 collective-permute-start.1
  28.2 2.1 collective-permute-done
  30.4 4.3 %collective-permute-done.1 = bf16[1,1,320,512]{3,2,1,0:T(8,128)(2,1)S(1)} collective-permute-done((bf16[1,1,320,512]{3,2,1,0:T(8,128)(2,1)S(1)}, bf16[1,1,320,512]{3,2,1,0:T(8,128)(2,1)S(1)}, u32[]{:S(2)}, u32[]{:S(2)}) %collective-permute-start.1) | collective-permute-done | bytes 327712 | tf_op jit(solution)/shard_map/ppermute | solution.py:17
  37.6 129.7 %all-reduce.1 = (f32[32,16]{1,0:T(8,128)S(1)}, f32[32,16]{1,0:T(8,128)S(1)}) all-reduce(f32[32,16]{1,0:T(8,128)S(1)} %reshape.178, f32[32,16]{1,0:T(8,128)S(1)} %reshape.177), channel_id=1, replica_groups=mesh['tm'=4,'rows'=64] {'tm','rows'}, use_global_device_ids=true, to_apply=%region_4.5 | all-reduce | flops 1024 | bytes 8192 | tf_op jit(solution)/shard_map/psum | solution.py:90
  167.8 3.9 fusion.113
  171.7 48.1 %conditional.1 = (f32[1,2,320,512]{3,2,1,0:T(8,128)}) conditional(s32[]{:T(128)} %convert_element_type.9, () %tuple.14, (bf16[3,4,322,512]{3,2,1,0:T(8,128)(2,1)}, bf16[3,3,3,512,512]{4,3,2,1,0:T(8,128)(2,1)}) %tuple.15), branch_computations={%region_6.7_spmd, %region_7.8_spmd} | conditional | flops 9124839424 | bytes 177053760 | solution.py:68
  171.7 1.9 convolution_bitcast_fusion.15
  173.7 1.8 convolution_bitcast_fusion.16
  175.5 1.7 convolution_bitcast_fusion.17
  177.2 2.0 convolution_bitcast_fusion.24
  179.2 2.1 convolution_bitcast_fusion.25
  202.4 1.7 convolution_bitcast_fusion.5
  210.8 9.0 %slice_add_fusion = f32[1,2,320,512]{3,2,1,0:T(8,128)} fusion(f32[1,2,322,512]{3,2,1,0:T(8,128)} %convolution_bitcast_fusion, f32[1,2,322,512]{3,2,1,0:T(8,128)} %convolution_bitcast_fusion.1, f32[1,2,322,512]{3,2,1,0:T(8,128)} %convolution_bitcast_fusion.2, f32[1,2,322,512]{3,2,1,0:T(8,128)} %convolution_bitcast_fusion.3, ...), kind=kLoop, calls=%fused_computation.27 | loop fusion | flops 8519680 | bytes 36700160 | tf_op jit(solution)/shard_map/cond/branch_1_fun/add | solution.py:47
  219.8 1.9 convolution_bitcast_fusion.28
  221.8 1.8 convolution_bitcast_fusion.27
  223.6 1.7 convolution_bitcast_fusion.31
  225.3 2.0 convolution_bitcast_fusion.30
  227.3 2.1 convolution_bitcast_fusion.34
  237.0 1.7 convolution_bitcast_fusion.45
  259.9 10.1 %fusion.115 = f32[320,512]{1,0:T(8,128)} fusion(f32[1,2,320,512]{3,2,1,0:T(8,128)} %get-tuple-element.36, f32[1,2,322,512]{3,2,1,0:T(8,128)S(1)} %convolution_bitcast_fusion.27, f32[1,2,322,512]{3,2,1,0:T(8,128)S(1)} %convolution_bitcast_fusion.28, f32[1,2,322,512]{3,2,1,0:T(8,128)} %convolution_bitcast_fusion.29, ...), kind=kLoop, calls=%fused_computation.198 | loop fusion | flops 9011200 | bytes 37355520 | tf_op jit(solution)/shard_map/reduce_sum | solution.py:53
  272.5 6.0 %all-reduce.3 = (f32[512]{0:T(512)S(1)}, f32[512]{0:T(512)S(1)}) all-reduce(f32[512]{0:T(512)S(1)} %get-tuple-element.18, f32[512]{0:T(512)S(1)} %get-tuple-element.17), channel_id=1, replica_groups=mesh['tm'=4,'rows'=64] {'tm'}, use_global_device_ids=true, to_apply=%region_15.16 | all-reduce | flops 1024 | bytes 8192 | tf_op jit(solution)/shard_map/psum | solution.py:103
  278.5 125.8 %all-reduce.2 = (f32[512]{0:T(512)S(1)}, f32[512]{0:T(512)S(1)}) all-reduce(f32[512]{0:T(512)S(1)} %get-tuple-element.25, f32[512]{0:T(512)S(1)} %get-tuple-element.26), channel_id=1, replica_groups=mesh['tm'=4,'rows'=64] {'rows'}, use_global_device_ids=true, to_apply=%region_16.17 | all-reduce | flops 1024 | bytes 8192 | tf_op jit(solution)/shard_map/psum | solution.py:102
  (94 shorter events, 65.5 us)
Async XLA Ops:
  7.2 23.2 %copy-start.4 = (bf16[1,2,320,512]{3,2,1,0:T(8,128)(2,1)S(1)}, bf16[1,2,320,512]{3,2,1,0:T(8,128)(2,1)}, u32[]{:S(2)}) copy-start(bf16[1,2,320,512]{3,2,1,0:T(8,128)(2,1)} %param.11) | copy-start | bytes 1966084
  7.2 164.5 %all-gather.2.cloned.1.call-start = ((), (), s32[]{:S(2)}) async-start(), calls=%async_computation | async-start | bytes 14376960 | tf_op jit(solution)/shard_map/all_gather | solution.py:85
  20.0 17.3 %copy-start.5 = (bf16[1,1,160,512]{3,2,1,0:T(8,128)(2,1)S(1)}, bf16[1,1,160,512]{3,2,1,0:T(8,128)(2,1)}, u32[]{:S(2)}) copy-start(bf16[1,1,160,512]{3,2,1,0:T(8,128)(2,1)} %param.7) | copy-start | bytes 491524
  20.1 10.2 %collective-permute-start = (bf16[1,1,320,512]{3,2,1,0:T(8,128)(2,1)S(1)}, bf16[1,1,320,512]{3,2,1,0:T(8,128)(2,1)S(1)}, u32[]{:S(2)}, u32[]{:S(2)}) collective-permute-start(bf16[1,1,320,512]{3,2,1,0:T(8,128)(2,1)S(1)} %get-tuple-element.29), channel_id=1, source_target_pairs={{0,1},{1,2},{2,3},{3,4},{4,5},{5,6},{6,7},{7,8},{8,9},{9,10},{10,1... | collective-permute-start | bytes 983048 | tf_op jit(solution)/shard_map/ppermute | solution.py:14
  26.3 8.4 %collective-permute-start.1 = (bf16[1,1,320,512]{3,2,1,0:T(8,128)(2,1)S(1)}, bf16[1,1,320,512]{3,2,1,0:T(8,128)(2,1)S(1)}, u32[]{:S(2)}, u32[]{:S(2)}) collective-permute-start(bf16[1,1,320,512]{3,2,1,0:T(8,128)(2,1)S(1)} %get-tuple-element.28), channel_id=1, source_target_pairs={{1,0},{2,1},{3,2},{4,3},{5,4},{6,5},{7,6},{8,7},{9,8},{10,9},{11,1... | collective-permute-start | bytes 983048 | tf_op jit(solution)/shard_map/ppermute | solution.py:17
  34.7 133.1 %collective-permute-start.3 = (bf16[1,4,320,512]{3,2,1,0:T(8,128)(2,1)S(1)}, bf16[1,4,320,512]{3,2,1,0:T(8,128)(2,1)}, u32[]{:S(2)}, u32[]{:S(2)}) collective-permute-start(bf16[1,4,320,512]{3,2,1,0:T(8,128)(2,1)S(1)} %constant_dynamic-update-slice_fusion), channel_id=1, source_target_pairs={{128,0},{192,64},{129,1},{193,65},{130,2},{194,66},{131,3},{195,67... | collective-permute-start | bytes 3932168 | tf_op jit(solution)/shard_map/ppermute | solution.py:25
  36.0 131.8 %collective-permute-start.2 = (bf16[1,4,320,512]{3,2,1,0:T(8,128)(2,1)S(1)}, bf16[1,4,320,512]{3,2,1,0:T(8,128)(2,1)}, u32[]{:S(2)}, u32[]{:S(2)}) collective-permute-start(bf16[1,4,320,512]{3,2,1,0:T(8,128)(2,1)S(1)} %constant_dynamic-update-slice_fusion), channel_id=1, source_target_pairs={{64,0},{128,64},{192,128},{65,1},{129,65},{193,129},{66,2},{130,66... | collective-permute-start | bytes 3932168 | tf_op jit(solution)/shard_map/ppermute | solution.py:25
  171.7 3.7 copy-start.1
  175.5 10.7 %copy-start.3 = (bf16[3,3,3,512,512]{4,3,2,1,0:T(8,128)(2,1)S(1)}, bf16[3,3,3,512,512]{4,3,2,1,0:T(8,128)(2,1)}, u32[]{:S(2)}) copy-start(bf16[3,3,3,512,512]{4,3,2,1,0:T(8,128)(2,1)} %get-tuple-element.13) | copy-start | bytes 42467332 | tf_op jit(solution)/shard_map/cond
  219.8 3.7 copy-start
  223.6 10.7 %copy-start.2 = (bf16[3,3,3,512,512]{4,3,2,1,0:T(8,128)(2,1)S(1)}, bf16[3,3,3,512,512]{4,3,2,1,0:T(8,128)(2,1)}, u32[]{:S(2)}) copy-start(bf16[3,3,3,512,512]{4,3,2,1,0:T(8,128)(2,1)} %all-gather.2.cloned.1.call-done) | copy-start | bytes 42467332
  270.0 2.3 copy-start.6
  270.0 2.3 copy-start.7
Sparse Core Ops, SparseCore 0:
  19.0 105.3 all-gather.1
